TPU v7x, 32 devices: a whole 2x2x4 slice. The times are simulated.
32 devices in a mesh: rep: 4 (over z), fsdp: 8 (over y, x, core).
Axes of the slice: x: 2, y: 2, z: 4, core: 2. Of those that a mesh axis runs over, the one named last changes fastest.
Arguments:
- activations: bfloat16 [4, 16384, 4096], P('rep', 'fsdp'), may hold values from -6 to 6
- cotangent: bfloat16 [4, 16384, 1024], P('rep', 'fsdp'), may hold values from -0.046875 to 0.046875
- momentum: float32 [4, 4096, 1024], P('rep', 'fsdp'), may hold values from -6 to 6
Outputs:
- momentum_next: float32 [4, 4096, 1024], P('rep', 'fsdp')
- update: float32 [4096, 1024], P('fsdp')
All inputs are finite; a program needn't handle non-finite values.
Results may differ from a plain program's by a relative error of at most 0.0021.
Values sent between devices are 32-bit elements; how exact they have to be, the bound alone decides.
No kernel may reach another device: no remote copies, remote signals or barrier semaphores. Data moves between devices by JAX's collectives and lax.ppermute only.
A program may use at most 128 MiB of HBM per device.

v0:
```python
import jax
import jax.numpy as jnp
from jax import lax
from jax.sharding import PartitionSpec as P

CH = 64
BAND = 16
momentum_decay = 0.9


def basis_rows(size, keep):
    freq = jnp.arange(keep, dtype=jnp.float32)[:, None]
    point = jnp.arange(size, dtype=jnp.float32)[None, :]
    waves = jnp.cos(jnp.pi * (2.0 * point + 1.0) * freq / (2.0 * size))
    scales = jnp.where(freq == 0.0, jnp.sqrt(1.0 / size), jnp.sqrt(2.0 / size))
    return waves * scales


def bands_of(field, basis):
    rows, width = field.shape
    blocks = field.reshape(rows // CH, CH, width // CH, CH)
    return jnp.einsum("kn,anbm,lm->akbl", basis, blocks, basis, precision=lax.Precision.HIGHEST)


def term_maker(normed, part):
    return lax.dot_general(
        normed, part, (((0,), (0,)), ((), ())), preferred_element_type=jnp.float32
    )


def settle(grad, field, basis):
    accumulated = momentum_decay * field + grad
    bands = bands_of(accumulated, basis)
    count, _, wide, _ = bands.shape
    blocks = jnp.einsum("kn,akbl,lm->anbm", basis, bands, basis, precision=lax.Precision.HIGHEST)
    return (accumulated - blocks.reshape(count * CH, wide * CH), bands)


def body(activations, cotangent, momentum):
    values = activations[0].astype(jnp.float32)
    stat = jnp.mean(values * values, axis=-1, keepdims=True)
    normed = (values * lax.rsqrt(stat + 1e-05)).astype(jnp.bfloat16)
    targets = cotangent[0]
    field = momentum[0]
    basis = basis_rows(CH, BAND)
    grad = lax.psum_scatter(term_maker(normed, targets), "fsdp", scatter_dimension=0, tiled=True)
    cleared, bands = settle(grad, field, basis)
    count, _, wide, _ = bands.shape
    summed = lax.psum(bands, "rep")
    blocks = jnp.einsum("kn,akbl,lm->anbm", basis, summed, basis, precision=lax.Precision.HIGHEST)
    update = blocks.reshape(count * CH, wide * CH)
    groups = lax.axis_size("rep")
    return (cleared[None], update / groups)


def solution(mesh):
    return jax.shard_map(
        body,
        mesh=mesh,
        in_specs=(P("rep", "fsdp", None), P("rep", "fsdp", None), P("rep", "fsdp", None)),
        out_specs=(P("rep", "fsdp", None), P("fsdp", None)),
        check_vma=False,
    )
```

profile of v0, /device:TPU:0, one launch (start us, length us, event | category | flops | bytes accessed | tf_op | source)
XLA Modules:
  0.0 262.0 jit_solution(10249392141727543123)
XLA Ops:
  7.2 0.0 reduce-scatter.2.cloned.1.call-start
  7.2 0.0 copy-start
  7.2 7.6 %fusion = f32[2048]{0:T(1024)S(1)} fusion(bf16[1,2048,4096]{2,1,0:T(8,128)(2,1)} %param.3), kind=kLoop, calls=%fused_computation.2 | loop fusion | flops 25163776 | bytes 16785408 | tf_op jit(solution)/shard_map/reduce_sum | solution.py:41
  14.8 3.1 %copy-done = bf16[1,2048,4096]{2,1,0:T(8,128)(2,1)S(1)} copy-done((bf16[1,2048,4096]{2,1,0:T(8,128)(2,1)S(1)}, bf16[1,2048,4096]{2,1,0:T(8,128)(2,1)}, u32[]{:S(2)}) %copy-start) | copy-done | bytes 16777240
  17.9 23.4 %fusion.3 = f32[4096,1024]{1,0:T(8,128)} fusion(bf16[1,2048,4096]{2,1,0:T(8,128)(2,1)S(1)} %copy-done, f32[2048]{0:T(1024)S(1)} %add_rsqrt_fusion, bf16[1,2048,1024]{2,1,0:T(8,128)(2,1)} %param.4), kind=kOutput, calls=%fused_computation.5 | convolution fusion | flops 17205035008 | bytes 37756928 | tf_op jit(solution)/shard_map/dot_general | solution.py:26
  41.3 0.0 reduce-scatter.2.cloned.1.call-update
  41.3 119.0 %reduce-scatter.2.cloned.1.call-done = f32[512,1024]{1,0:T(8,128)} async-done(((f32[4096,1024]{1,0:T(8,128)}), f32[512,1024]{1,0:T(8,128)}) %reduce-scatter.2.cloned.1.call-update) | async-done | bytes 2097168 | tf_op jit(solution)/shard_map/reduce_scatter | solution.py:46
  160.3 2.7 %bitcast_add_fusion = f32[512,1024]{1,0:T(8,128)S(1)} fusion(f32[512,1024]{1,0:T(8,128)} %reduce-scatter.2.cloned.1.call-done, f32[1,512,1024]{2,1,0:T(8,128)} %param.5), kind=kLoop, calls=%fused_computation.12 | loop fusion | flops 1048576 | bytes 6291456 | tf_op jit(solution)/shard_map/add | solution.py:32
  163.0 2.5 reshape.49
  165.5 5.6 %fusion.7 = f32[8,16,64,16]{2,3,1,0:T(8,128)S(1)} fusion(f32[8,64,16,64]{3,2,1,0:T(8,128)} %reshape.49, f32[16]{0:T(128)S(1)} %compare_select_fusion, f32[64]{0:T(128)S(1)} %add_multiply_fusion), kind=kOutput, calls=%fused_computation.8 | convolution fusion | flops 100666368 | bytes 2621760 | tf_op jit(solution)/shard_map/kn,anbm,lm->akbl/dot_general | solution.py:22
  171.1 1.0 convolution_bitcast_fusion.1
  172.1 2.8 %fusion.13 = f32[8,16,16,64]{3,2,1,0:T(8,128)} fusion(f32[8,16,16,16]{3,1,2,0:T(8,128)S(1)} %convolution_bitcast_fusion.1, f32[16]{0:T(128)S(1)} %compare_select_fusion, f32[64]{0:T(128)S(1)} %add_multiply_fusion), kind=kOutput, calls=%fused_computation.19 | convolution fusion | flops 25168896 | bytes 655680 | tf_op jit(solution)/shard_map/kn,akbl,lm->anbm/dot_general | solution.py:35
  174.9 0.0 all-reduce.2.cloned.1.call-start
  174.9 9.3 %convolution_bitcast_fusion = f32[8,64,16,64]{3,1,2,0:T(8,128)} fusion(f32[8,16,16,64]{3,2,1,0:T(8,128)} %fusion.13, f32[16]{0:T(128)S(1)} %compare_select_fusion, f32[64]{0:T(128)S(1)} %add_multiply_fusion), kind=kOutput, calls=%fused_computation.11 | convolution fusion | flops 100666368 | bytes 2621760 | tf_op jit(solution)/shard_map/kn,akbl,lm->anbm/dot_general | solution.py:35
  184.2 0.0 copy-done.1
  184.2 0.0 all-reduce.2.cloned.1.call-update
  184.2 6.5 %copy.6 = f32[8,64,16,64]{3,2,1,0:T(8,128)} copy(f32[8,64,16,64]{3,1,2,0:T(8,128)} %convolution_bitcast_fusion) | data formatting | bytes 4194304 | tf_op jit(solution)/shard_map/kn,akbl,lm->anbm/transpose | solution.py:35
  190.8 4.8 %reshape.50 = f32[512,1024]{1,0:T(8,128)} reshape(f32[8,64,16,64]{3,2,1,0:T(8,128)} %copy.6) | data formatting | bytes 4194304 | tf_op jit(solution)/shard_map/reshape | solution.py:36
  195.6 3.3 %subtract_bitcast_fusion = f32[1,512,1024]{2,1,0:T(8,128)} fusion(f32[512,1024]{1,0:T(8,128)S(1)} %bitcast_add_fusion, f32[512,1024]{1,0:T(8,128)} %reshape.50), kind=kLoop, calls=%fused_computation.13 | loop fusion | flops 524288 | bytes 6291456 | tf_op jit(solution)/shard_map/broadcast_in_dim | solution.py:53
  198.9 37.4 %all-reduce.2.cloned.1.call-done = f32[8,16,16,16]{3,1,2,0:T(8,128)} async-done(((f32[8,16,16,16]{3,1,2,0:T(8,128)}), f32[8,16,16,16]{3,1,2,0:T(8,128)}) %all-reduce.2.cloned.1.call-update) | async-done | bytes 131088 | tf_op jit(solution)/shard_map/psum | solution.py:49
  236.3 3.0 %fusion.10 = f32[8,16,16,64]{3,2,1,0:T(8,128)S(1)} fusion(f32[8,16,16,16]{3,1,2,0:T(8,128)} %all-reduce.2.cloned.1.call-done, f32[16]{0:T(128)S(1)} %compare_select_fusion, f32[64]{0:T(128)S(1)} %add_multiply_fusion), kind=kOutput, calls=%fused_computation.16 | convolution fusion | flops 25168896 | bytes 655680 | tf_op jit(solution)/shard_map/kn,akbl,lm->anbm/dot_general | solution.py:50
  239.3 6.7 %multiply_bitcast_fusion = f32[8,64,16,64]{3,1,2,0:T(8,128)S(1)} fusion(f32[8,16,16,64]{3,2,1,0:T(8,128)S(1)} %fusion.10, f32[16]{0:T(128)S(1)} %compare_select_fusion, f32[64]{0:T(128)S(1)} %add_multiply_fusion), kind=kOutput, calls=%fused_computation.10 | convolution fusion | flops 101190656 | bytes 2621760 | tf_op jit(solution)/shard_map/kn,akbl,lm->anbm/dot_general | solution.py:50
  246.1 4.3 %copy.7 = f32[8,64,16,64]{3,2,1,0:T(8,128)} copy(f32[8,64,16,64]{3,1,2,0:T(8,128)S(1)} %multiply_bitcast_fusion) | data formatting | bytes 4194304 | tf_op jit(solution)/shard_map/div | solution.py:53
  250.4 4.8 %div.39 = f32[512,1024]{1,0:T(8,128)} reshape(f32[8,64,16,64]{3,2,1,0:T(8,128)} %copy.7) | data formatting | bytes 4194304 | tf_op jit(solution)/shard_map/div | solution.py:53
  (4 shorter events, 0.0 us)
Async XLA Ops:
  7.2 153.2 %reduce-scatter.2.cloned.1.call-start = ((), (), s32[]{:S(2)}) async-start(), calls=%async_computation.1 | async-start | bytes 18874368 | tf_op jit(solution)/shard_map/reduce_scatter | solution.py:46
  7.2 10.7 %copy-start = (bf16[1,2048,4096]{2,1,0:T(8,128)(2,1)S(1)}, bf16[1,2048,4096]{2,1,0:T(8,128)(2,1)}, u32[]{:S(2)}) copy-start(bf16[1,2048,4096]{2,1,0:T(8,128)(2,1)} %param.3) | copy-start | bytes 50331652
  172.1 12.1 %copy-start.1 = (f32[8,16,16,16]{3,1,2,0:T(8,128)}, f32[8,16,16,16]{3,1,2,0:T(8,128)S(1)}, u32[]{:S(2)}) copy-start(f32[8,16,16,16]{3,1,2,0:T(8,128)S(1)} %convolution_bitcast_fusion.1) | copy-start | bytes 393220
  174.9 61.4 %all-reduce.2.cloned.1.call-start = ((), (), s32[]{:S(2)}) async-start(), calls=%async_computation.2 | async-start | bytes 2097152 | tf_op jit(solution)/shard_map/psum | solution.py:49
Sparse Core Ops, SparseCore 0:
  41.4 118.8 reduce-scatter.1
  184.4 51.8 all-reduce.1
where the time goes:
time: 262 us
  waiting for transfers between devices  156 us (60%)
  matrix products  51.8 us (20%)
  local copies, waits for them, and re-layouts  26.1 us (10%)
  between operations  14.1 us (5%)
  other arithmetic  13.6 us (5%)
    reduce_scatter x1, waiting for transfers between devices, body(): lax.psum_scatter(term_maker(normed, targets), 'fsdp', scatter_dimension=0...  119 us
    psum x1, waiting for transfers between devices, body(): summed = lax.psum(bands, 'rep')  37.4 us
    dot_general x1, matrix products, term_maker(): lax.dot_general(normed, part, (((0,), (0,)), ((), ())), preferred_element...  23.4 us
    dot_general x2, matrix products, settle(): jnp.einsum('kn,akbl,lm->anbm', basis, bands, basis, precision=lax.Precisi...  12.1 us
    dot_general x2, matrix products, body(): jnp.einsum('kn,akbl,lm->anbm', basis, summed, basis, precision=lax.Precis...  9.76 us
    div x2, local copies, waits for them, and re-layouts, body(): return (cleared[None], update / groups)  9.14 us
    reduce_sum x1, other arithmetic, body(): stat = jnp.mean(values * values, axis=-1, keepdims=True)  7.6 us
    dot_general x2, matrix products, bands_of(): jnp.einsum('kn,anbm,lm->akbl', basis, blocks, basis, precision=lax.Precis...  6.6 us
  transfers between devices with their start and end apart: 2, of which 2 were waited for; matrix products, arithmetic and copies ran while one was open for 6% of the time, Pallas kernels for 0%

commit v1 on v0

--- a/solution.py
+++ b/solution.py
@@ -46,7 +46,8 @@
     grad = lax.psum_scatter(term_maker(normed, targets), "fsdp", scatter_dimension=0, tiled=True)
     cleared, bands = settle(grad, field, basis)
     count, _, wide, _ = bands.shape
-    summed = lax.psum(bands, "rep")
+    terms = lax.all_gather(bands, "rep")
+    summed = jnp.sum(terms, axis=0)
     blocks = jnp.einsum("kn,akbl,lm->anbm", basis, summed, basis, precision=lax.Precision.HIGHEST)
     update = blocks.reshape(count * CH, wide * CH)
     groups = lax.axis_size("rep")

time: 262 us -> 293 us (1.12)
  blocking collectives: 0 us -> 71.6 us
  waiting for transfers between devices: 156 us -> 119 us
  matrix products: 51.8 us -> 47.3 us
    all_gather x0 -> x1, blocking collectives: none -> 71.6 us  [body(): terms = lax.all_gather(bands, 'rep')]
    psum x1 -> x0, waiting for transfers between devices: 37.4 us -> none  [body(): summed = lax.psum(bands, 'rep')]
    dot_general x2, matrix products: 12.1 us -> 8.54 us  [settle(): jnp.einsum('kn,akbl,lm->anbm', basis, bands, basis, precision=lax.Precisi...]
  transfers between devices with their start and end apart: 2 -> 1, of which waited for: 2 -> 1; matrix products, arithmetic and copies ran while one was open for 6% -> 0% of each run, Pallas kernels for 0% -> 0%
where the time goes in v1:
time: 293 us
  waiting for transfers between devices  119 us (41%)
  blocking collectives  71.6 us (24%)
  matrix products  47.3 us (16%)
  local copies, waits for them, and re-layouts  24.2 us (8%)
  other arithmetic  16.3 us (6%)
  between operations  14.1 us (5%)
    reduce_scatter x1, waiting for transfers between devices, body(): lax.psum_scatter(term_maker(normed, targets), 'fsdp', scatter_dimension=0...  119 us
    all_gather x1, blocking collectives, body(): terms = lax.all_gather(bands, 'rep')  71.6 us
    dot_general x1, matrix products, term_maker(): lax.dot_general(normed, part, (((0,), (0,)), ((), ())), preferred_element...  23.4 us
    div x2, local copies, waits for them, and re-layouts, body(): return (cleared[None], update / groups)  9.14 us
    dot_general x2, matrix products, body(): jnp.einsum('kn,akbl,lm->anbm', basis, summed, basis, precision=lax.Precis...  8.65 us
    dot_general x2, matrix products, settle(): jnp.einsum('kn,akbl,lm->anbm', basis, bands, basis, precision=lax.Precisi...  8.54 us
    reduce_sum x1, other arithmetic, body(): stat = jnp.mean(values * values, axis=-1, keepdims=True)  7.6 us
    dot_general x2, matrix products, bands_of(): jnp.einsum('kn,anbm,lm->akbl', basis, blocks, basis, precision=lax.Precis...  6.78 us
  transfers between devices with their start and end apart: 1, of which 1 were waited for; matrix products, arithmetic and copies ran while one was open for 0% of the time, Pallas kernels for 0%

profile of v1, /device:TPU:0, one launch (start us, length us, event | category | flops | bytes accessed | tf_op | source)
XLA Modules:
  0.0 292.6 jit_solution(11358705074118501277)
XLA Ops:
  7.2 0.0 reduce-scatter.2.cloned.1.call-start
  7.2 0.0 copy-start
  7.2 7.6 %fusion = f32[2048]{0:T(1024)S(1)} fusion(bf16[1,2048,4096]{2,1,0:T(8,128)(2,1)} %param.3), kind=kLoop, calls=%fused_computation.2 | loop fusion | flops 25163776 | bytes 16785408 | tf_op jit(solution)/shard_map/reduce_sum | solution.py:41
  14.8 3.1 %copy-done = bf16[1,2048,4096]{2,1,0:T(8,128)(2,1)S(1)} copy-done((bf16[1,2048,4096]{2,1,0:T(8,128)(2,1)S(1)}, bf16[1,2048,4096]{2,1,0:T(8,128)(2,1)}, u32[]{:S(2)}) %copy-start) | copy-done | bytes 16777240
  17.9 23.4 %fusion.3 = f32[4096,1024]{1,0:T(8,128)} fusion(bf16[1,2048,4096]{2,1,0:T(8,128)(2,1)S(1)} %copy-done, f32[2048]{0:T(1024)S(1)} %add_rsqrt_fusion, bf16[1,2048,1024]{2,1,0:T(8,128)(2,1)} %param.4), kind=kOutput, calls=%fused_computation.5 | convolution fusion | flops 17205035008 | bytes 37756928 | tf_op jit(solution)/shard_map/dot_general | solution.py:26
  41.3 0.0 reduce-scatter.2.cloned.1.call-update
  41.3 119.0 %reduce-scatter.2.cloned.1.call-done = f32[512,1024]{1,0:T(8,128)} async-done(((f32[4096,1024]{1,0:T(8,128)}), f32[512,1024]{1,0:T(8,128)}) %reduce-scatter.2.cloned.1.call-update) | async-done | bytes 2097168 | tf_op jit(solution)/shard_map/reduce_scatter | solution.py:46
  160.3 2.7 bitcast_add_fusion
  163.0 2.5 reshape.49
  165.5 5.8 %fusion.7 = f32[8,16,64,16]{2,3,1,0:T(8,128)S(1)} fusion(f32[8,64,16,64]{3,2,1,0:T(8,128)} %reshape.49, f32[16]{0:T(128)S(1)} %compare_select_fusion, f32[64]{0:T(128)S(1)} %add_multiply_fusion), kind=kOutput, calls=%fused_computation.8 | convolution fusion | flops 100666368 | bytes 2621760 | tf_op jit(solution)/shard_map/kn,anbm,lm->akbl/dot_general | solution.py:22
  171.3 1.0 convolution_bitcast_fusion.1
  172.3 1.8 fusion.14
  174.1 0.3 copy.11
  174.4 6.7 %convolution_bitcast_fusion = f32[8,64,16,64]{3,1,2,0:T(8,128)S(1)} fusion(f32[8,16,16,64]{3,2,1,0:T(8,128)S(1)} %fusion.14, f32[16]{0:T(128)S(1)} %compare_select_fusion, f32[64]{0:T(128)S(1)} %add_multiply_fusion), kind=kOutput, calls=%fused_computation.11 | convolution fusion | flops 100666368 | bytes 2621760 | tf_op jit(solution)/shard_map/kn,akbl,lm->anbm/dot_general | solution.py:35
  181.2 4.3 %copy.10 = f32[8,64,16,64]{3,2,1,0:T(8,128)} copy(f32[8,64,16,64]{3,1,2,0:T(8,128)S(1)} %convolution_bitcast_fusion) | data formatting | bytes 4194304 | tf_op jit(solution)/shard_map/kn,akbl,lm->anbm/transpose | solution.py:35
  185.5 4.8 %reshape.50 = f32[512,1024]{1,0:T(8,128)} reshape(f32[8,64,16,64]{3,2,1,0:T(8,128)} %copy.10) | data formatting | bytes 4194304 | tf_op jit(solution)/shard_map/reshape | solution.py:36
  190.3 3.3 %subtract_bitcast_fusion = f32[1,512,1024]{2,1,0:T(8,128)} fusion(f32[512,1024]{1,0:T(8,128)S(1)} %bitcast_add_fusion, f32[512,1024]{1,0:T(8,128)} %reshape.50), kind=kLoop, calls=%fused_computation.13 | loop fusion | flops 524288 | bytes 6291456 | tf_op jit(solution)/shard_map/broadcast_in_dim | solution.py:54
  193.6 71.6 %all-gather = f32[32,16,16,16]{3,2,1,0:T(8,128)} all-gather(f32[8,16,16,16]{3,2,1,0:T(8,128)S(1)} %copy.11), channel_id=2, replica_groups=mesh['rep'=4,'fsdp'=8] {'rep'}, dimensions={0}, use_global_device_ids=true | all-gather | bytes 655360 | tf_op jit(solution)/shard_map/all_gather | solution.py:49
  265.2 2.7 reduce_sum.19
  267.9 1.9 fusion.9
  269.8 6.7 %multiply_bitcast_fusion = f32[8,64,16,64]{3,1,2,0:T(8,128)S(1)} fusion(f32[8,16,16,64]{3,2,1,0:T(8,128)S(1)} %fusion.9, f32[16]{0:T(128)S(1)} %compare_select_fusion, f32[64]{0:T(128)S(1)} %add_multiply_fusion), kind=kOutput, calls=%fused_computation.10 | convolution fusion | flops 101190656 | bytes 2621760 | tf_op jit(solution)/shard_map/kn,akbl,lm->anbm/dot_general | solution.py:51
  276.6 4.3 %copy.14 = f32[8,64,16,64]{3,2,1,0:T(8,128)} copy(f32[8,64,16,64]{3,1,2,0:T(8,128)S(1)} %multiply_bitcast_fusion) | data formatting | bytes 4194304 | tf_op jit(solution)/shard_map/div | solution.py:54
  280.9 4.8 %div.39 = f32[512,1024]{1,0:T(8,128)} reshape(f32[8,64,16,64]{3,2,1,0:T(8,128)} %copy.14) | data formatting | bytes 4194304 | tf_op jit(solution)/shard_map/div | solution.py:54
  (3 shorter events, 0.0 us)
Async XLA Ops:
  7.2 153.2 %reduce-scatter.2.cloned.1.call-start = ((), (), s32[]{:S(2)}) async-start(), calls=%async_computation.1 | async-start | bytes 18874368 | tf_op jit(solution)/shard_map/reduce_scatter | solution.py:46
  7.2 10.7 %copy-start = (bf16[1,2048,4096]{2,1,0:T(8,128)(2,1)S(1)}, bf16[1,2048,4096]{2,1,0:T(8,128)(2,1)}, u32[]{:S(2)}) copy-start(bf16[1,2048,4096]{2,1,0:T(8,128)(2,1)} %param.3) | copy-start | bytes 50331652
Sparse Core Ops, SparseCore 0:
  41.4 118.8 reduce-scatter.1
